TPU v7x, 32 devices: a whole 2x2x4 slice. The times are simulated.
32 devices in a mesh: dp: 4 (over y, core), row: 2 (over x), col: 4 (over z).
Axes of the slice: x: 2, y: 2, z: 4, core: 2. Of those that a mesh axis runs over, the one named last changes fastest.
Arguments:
- inputs: bfloat16 [2048, 6144], P('dp', 'row'), may hold values from -600 to 600
- saved_qkv: bfloat16 [2048, 3, 3072], P('dp', None, 'col'), may hold values from -6 to 6
- saved_up: bfloat16 [2048, 12288], P('dp', 'col'), may hold values from -6 to 6
- cotangent: bfloat16 [2048, 6144], P('dp', 'row'), may hold values from -6 to 6
- weight_qkv: bfloat16 [6144, 3, 3072], P('row', None, 'col'), may hold values from -0.078125 to 0.078125
- weight_up: bfloat16 [6144, 12288], P('row', 'col'), may hold values from -0.078125 to 0.078125
- weight_attn: bfloat16 [3072, 6144], P('col', 'row'), may hold values from -0.109375 to 0.109375
- weight_down: bfloat16 [12288, 6144], P('col', 'row'), may hold values from -0.0546875 to 0.0546875
Outputs:
- grad_inputs: bfloat16 [2048, 6144], P(('dp', 'col'), 'row')
- grad_qkv: bfloat16 [2, 4, 768, 3, 3072], P('row', 'dp', None, None, 'col')
- grad_up: bfloat16 [2, 4, 768, 12288], P('row', 'dp', None, 'col')
- grad_attn: bfloat16 [4, 4, 192, 6144], P('col', 'dp', None, 'row')
- grad_down: bfloat16 [4, 4, 768, 6144], P('col', 'dp', None, 'row')
All inputs are finite; a program needn't handle non-finite values.
Results may differ from a plain program's by a relative error of at most 0.0039.
The roundings to bfloat16 on the way count: a program that leaves them out, or rounds other values in their place, can miss the bound.
Values may be sent and summed in bfloat16 or wider, within the bound.
No kernel may reach another device: no remote copies, remote signals or barrier semaphores. Data moves between devices by JAX's collectives and lax.ppermute only.
A program may use at most 192 MiB of HBM per device.

v0:
```python
import jax
import jax.numpy as jnp
from jax import lax
from jax.sharding import PartitionSpec as P

HD = 128
S = 256
EPS = 1e-06
SQRT_HALF = 0.7071067811865476
INV_ROOT_TWO_PI = 0.3989422804014327


def gelu_exact(values):
    return 0.5 * values * (1.0 + jax.scipy.special.erf(values * SQRT_HALF))


def gelu_slope(values):
    cumul = 0.5 * (1.0 + jax.scipy.special.erf(values * SQRT_HALF))
    return cumul + values * jnp.exp(-0.5 * values * values) * INV_ROOT_TWO_PI


def head_norm(values):
    average = jnp.mean(values, axis=-1, keepdims=True)
    centred = values - average
    inv_std = lax.rsqrt(jnp.mean(centred * centred, axis=-1, keepdims=True) + EPS)
    return (centred * inv_std, inv_std)


def head_norm_back(normed, inv_std, upstream):
    first = jnp.mean(upstream, axis=-1, keepdims=True)
    cross = jnp.mean(upstream * normed, axis=-1, keepdims=True)
    return inv_std * (upstream - first - normed * cross)


def body(inputs, saved_qkv, saved_up, cotangent, weight_qkv, weight_up, weight_attn, weight_down):
    f32 = jnp.float32
    bf16 = jnp.bfloat16
    tok_rows, feat_local = inputs.shape
    head_cols = saved_qkv.shape[2]
    up_cols = saved_up.shape[1]
    n_row = lax.axis_size("row")
    n_col = lax.axis_size("col")
    width = feat_local * n_row
    head_count = head_cols // HD
    images = tok_rows // S
    values = inputs.astype(f32)
    first_sum, square_sum = lax.psum(
        (jnp.sum(values, axis=1), jnp.sum(values * values, axis=1)), "row"
    )
    average = (first_sum / width)[:, None]
    inv_std = lax.rsqrt((square_sum / width)[:, None] - average * average + EPS)
    normed = (values - average) * inv_std
    normed_b = normed.astype(bf16)
    qkv5 = saved_qkv.reshape(images, S, 3, head_count, HD)
    query = qkv5[:, :, 0]
    keyed = qkv5[:, :, 1]
    valued = qkv5[:, :, 2]
    q_norm, q_inv = head_norm(query.astype(f32))
    k_norm, k_inv = head_norm(keyed.astype(f32))
    qn_b = q_norm.astype(bf16)
    kn_b = k_norm.astype(bf16)
    scale = HD ** (-0.5)
    scores = jnp.einsum("bqhd,bkhd->bhqk", qn_b, kn_b, preferred_element_type=f32) * scale
    expo = jnp.exp(scores)
    probs = expo / jnp.sum(expo, axis=-1, keepdims=True)
    probs_b = probs.astype(bf16)
    attended = jnp.einsum("bhqk,bkhd->bqhd", probs_b, valued, preferred_element_type=f32).astype(
        bf16
    )
    attended = attended.reshape(tok_rows, head_cols)
    hidden_b = gelu_exact(saved_up.astype(f32)).astype(bf16)
    part_attn = jnp.einsum("td,ad->ta", cotangent, weight_attn, preferred_element_type=f32)
    part_hidden = jnp.einsum("td,fd->tf", cotangent, weight_down, preferred_element_type=f32)
    sum_attn, sum_hidden = lax.psum((part_attn, part_hidden), "row")
    grad_o = sum_attn.astype(bf16)
    grad_pre = (sum_hidden * gelu_slope(saved_up.astype(f32))).astype(bf16)
    grad_o4 = grad_o.reshape(images, S, head_count, HD)
    grad_probs = jnp.einsum("bqhd,bkhd->bhqk", grad_o4, valued, preferred_element_type=f32)
    grad_value = jnp.einsum("bhqk,bqhd->bkhd", probs_b, grad_o4, preferred_element_type=f32).astype(
        bf16
    )
    rowdot = jnp.sum(probs * grad_probs, axis=-1, keepdims=True)
    grad_scores = (probs * (grad_probs - rowdot) * scale).astype(bf16)
    grad_qn = jnp.einsum("bhqk,bkhd->bqhd", grad_scores, kn_b, preferred_element_type=f32)
    grad_kn = jnp.einsum("bhqk,bqhd->bkhd", grad_scores, qn_b, preferred_element_type=f32)
    grad_query = head_norm_back(q_norm, q_inv, grad_qn).astype(bf16)
    grad_key = head_norm_back(k_norm, k_inv, grad_kn).astype(bf16)
    grad_flat = jnp.stack([grad_query, grad_key, grad_value], axis=2).reshape(
        tok_rows, 3 * head_cols
    )
    flat_weight = weight_qkv.reshape(feat_local, 3 * head_cols)
    share_rows = tok_rows // n_col
    total = jnp.einsum("ta,da->td", grad_flat, flat_weight, preferred_element_type=f32)
    grad_normed = lax.psum_scatter(
        total + jnp.einsum("tf,df->td", grad_pre, weight_up, preferred_element_type=f32),
        "col",
        scatter_dimension=0,
        tiled=True,
    )
    first_row = lax.axis_index("col") * share_rows
    normed_share = lax.dynamic_slice_in_dim(normed, first_row, share_rows, 0)
    inv_share = lax.dynamic_slice_in_dim(inv_std, first_row, share_rows, 0)
    cot_share = lax.dynamic_slice_in_dim(cotangent, first_row, share_rows, 0)
    sum_grad, sum_cross = lax.psum(
        (jnp.sum(grad_normed, axis=1), jnp.sum(grad_normed * normed_share, axis=1)), "row"
    )
    branch_term = (
        grad_normed - (sum_grad / width)[:, None] - normed_share * (sum_cross / width)[:, None]
    )
    grad_inputs = (cot_share.astype(f32) + inv_share * branch_term).astype(bf16)
    moved_normed, moved_attended, moved_hidden = (
        lax.all_to_all(normed_b, "dp", split_axis=1, concat_axis=0, tiled=True),
        lax.all_to_all(attended, "dp", split_axis=1, concat_axis=0, tiled=True),
        lax.all_to_all(hidden_b, "dp", split_axis=1, concat_axis=0, tiled=True),
    )
    cot_piece = lax.all_gather(cotangent, "dp", axis=0, tiled=True)
    flat_piece = lax.all_gather(grad_flat, "dp", axis=0, tiled=True)
    pre_piece = lax.all_gather(grad_pre, "dp", axis=0, tiled=True)
    new_qkv = jnp.einsum("td,ta->da", moved_normed, flat_piece, preferred_element_type=f32)
    new_up = jnp.einsum("td,tf->df", moved_normed, pre_piece, preferred_element_type=f32)
    new_attn = jnp.einsum("ta,td->ad", moved_attended, cot_piece, preferred_element_type=f32)
    new_down = jnp.einsum("tf,td->fd", moved_hidden, cot_piece, preferred_element_type=f32)
    grad_qkv = new_qkv.astype(bf16).reshape(1, 1, new_qkv.shape[0], 3, head_cols)
    grad_up = new_up.astype(bf16).reshape(1, 1, new_up.shape[0], up_cols)
    grad_attn = new_attn.astype(bf16).reshape(1, 1, new_attn.shape[0], feat_local)
    grad_down = new_down.astype(bf16).reshape(1, 1, new_down.shape[0], feat_local)
    return (grad_inputs, grad_qkv, grad_up, grad_attn, grad_down)


def solution(mesh):
    return jax.shard_map(
        body,
        mesh=mesh,
        in_specs=(
            P("dp", "row"),
            P("dp", None, "col"),
            P("dp", "col"),
            P("dp", "row"),
            P("row", None, "col"),
            P("row", "col"),
            P("col", "row"),
            P("col", "row"),
        ),
        out_specs=(
            P(("dp", "col"), "row"),
            P("row", "dp", None, None, "col"),
            P("row", "dp", None, "col"),
            P("col", "dp", None, "row"),
            P("col", "dp", None, "row"),
        ),
        check_vma=False,
    )
```

profile of v0, /device:TPU:0, one launch (start us, length us, event | category | flops | bytes accessed | tf_op | source)
XLA Modules:
  0.0 490.4 jit_solution(17388915969645549124)
XLA Ops:
  8.0 0.0 all-reduce.5.cloned.1.call-start
  8.0 16.4 %fusion.87 = f32[512,3072]{1,0:T(8,128)} fusion(bf16[512,3072]{1,0:T(8,128)(2,1)} %param.11, bf16[3072,3072]{1,0:T(8,128)(2,1)} %param.15), kind=kOutput, calls=%fused_computation.110 | convolution fusion | flops 9663676416 | bytes 28311552 | tf_op jit(solution)/shard_map/td,fd->tf/dot_general | solution.py:73
  24.5 0.0 all-gather.4.cloned.1.call-start
  24.5 7.2 %fusion.85 = f32[512,768]{1,0:T(8,128)} fusion(bf16[512,3072]{1,0:T(8,128)(2,1)} %param.11, bf16[768,3072]{1,0:T(8,128)(2,1)} %param.14), kind=kOutput, calls=%fused_computation.108 | convolution fusion | flops 2415919104 | bytes 9437184 | tf_op jit(solution)/shard_map/td,ad->ta/dot_general | solution.py:72
  31.7 1.0 convert_reduce_fusion
  32.7 79.4 %all-reduce.6 = (bf16[512,768]{1,0:T(8,128)(2,1)S(1)}, f32[512]{0:T(512)S(1)}, f32[512]{0:T(512)S(1)}) all-reduce(f32[512,768]{1,0:T(8,128)} %fusion.85, f32[512]{0:T(512)S(1)} %get-tuple-element.16, f32[512]{0:T(512)S(1)} %get-tuple-element.15), channel_id=1, replica_groups=mesh['dp'=4,'row'=2,'col'=4] {'row'}, use_global_device_ids=true, to_apply=%region_9.0 | all-reduce | flops 394240 | bytes 2367488 | tf_op jit(solution)/shard_map/psum | solution.py:74
  112.2 0.9 reshape.107
  113.1 0.6 copy.35
  113.7 2.8 copy.25
  116.5 2.1 reshape.99
  118.7 3.8 fusion.80
  122.4 2.5 copy.54
  124.9 0.2 convert_reduce_fusion.1
  125.1 0.2 fusion.47
  125.3 0.2 fusion.36
  125.6 2.2 fusion.55
  127.8 2.5 fusion.17
  130.4 7.8 %bitcast_reduce_fusion = (f32[2,256,6]{1,2,0:T(8,128)S(1)}, f32[2,256,6]{1,2,0:T(8,128)S(1)}, f32[2,6,128,256]{3,2,1,0:T(8,128)}) fusion(f32[2,256,6]{1,2,0:T(8,128)S(1)} %add_rsqrt_fusion, f32[2,256,6]{1,2,0:T(8,128)S(1)} %broadcast_multiply_fusion.4, bf16[2,256,1,6,128]{1,0,4,3,2:T(2,128)(2,1)S(1)} %get-tuple-element.34, f32[2,6,256,256]{2,3,1,0:T(8,128)} %fusion.55, ...), kind=kOutput, calls=%fused_computation.66 | convolution fusion | flops 212333824 | bytes 9523200 | tf_op jit(solution)/shard_map/bhqk,bqhd->bkhd/dot_general | solution.py:85
  138.2 7.7 %bitcast_reduce_fusion.1 = (f32[2,256,6]{1,2,0:T(8,128)S(1)}, f32[2,256,6]{1,2,0:T(8,128)S(1)}, f32[2,6,128,256]{3,2,1,0:T(8,128)}) fusion(f32[2,256,6]{1,2,0:T(8,128)S(1)} %add_rsqrt_fusion.1, f32[2,256,6]{1,2,0:T(8,128)S(1)} %broadcast_multiply_fusion.5, bf16[2,256,1,6,128]{1,0,4,3,2:T(2,128)(2,1)S(1)} %get-tuple-element.33, ...), kind=kOutput, calls=%fused_computation.68 | convolution fusion | flops 212333824 | bytes 9523200 | tf_op jit(solution)/shard_map/bhqk,bkhd->bqhd/dot_general | solution.py:84
  145.9 2.1 fusion.52
  148.1 0.1 copy-done.8
  148.2 0.4 fusion.53
  148.6 0.7 copy-done.10
  149.2 0.8 fusion.50
  150.0 0.3 pad_maximum_fusion
  150.3 2.4 copy.37
  152.7 1.9 copy.60
  154.6 0.0 all-gather.4.cloned.1.call-update
  154.6 0.0 reduce-scatter.2.cloned.1.call-start
  154.7 19.4 %copy.38 = bf16[3072,3,768]{0,2,1:T(8,128)(2,1)} copy(bf16[3072,3,768]{2,0,1:T(8,128)(2,1)} %param.12) | data formatting | bytes 28311552 | tf_op args[4]
  174.1 12.6 %fusion.86 = f32[512,3072]{1,0:T(8,128)} fusion(bf16[512,2304]{0,1:T(8,128)(2,1)S(1)} %bitcast.152, bf16[3072,2304]{0,1:T(8,128)(2,1)} %bitcast.147), kind=kOutput, calls=%fused_computation.109 | convolution fusion | flops 7247757312 | bytes 22806528 | tf_op jit(solution)/shard_map/ta,da->td/dot_general | solution.py:93
  186.7 27.9 %all-reduce.5.cloned.1.call-done = f32[512,3072]{1,0:T(8,128)} async-done(((f32[512,3072]{1,0:T(8,128)}), f32[512,3072]{1,0:T(8,128)}) %all-reduce.5.cloned.1.call-update) | async-done | bytes 6291472 | tf_op jit(solution)/shard_map/psum | solution.py:74
  214.6 7.8 %fusion.11 = (bf16[512,3072]{1,0:T(8,128)(2,1)}, bf16[512,3072]{1,0:T(8,128)(2,1)S(1)}) fusion(bf16[512,3072]{1,0:T(8,128)(2,1)} %param.10, f32[512,3072]{1,0:T(8,128)} %all-reduce.5.cloned.1.call-done), kind=kLoop, calls=%fused_computation.19 | loop fusion | flops 22020096 | bytes 15728640 | tf_op jit(solution)/shard_map/convert_element_type | solution.py:71
  222.4 17.5 %convolution_add_fusion = f32[512,3072]{1,0:T(8,128)} fusion(f32[512,3072]{1,0:T(8,128)} %fusion.86, bf16[512,3072]{1,0:T(8,128)(2,1)S(1)} %get-tuple-element.31, bf16[3072,3072]{1,0:T(8,128)(2,1)} %param.13), kind=kOutput, calls=%fused_computation.23 | convolution fusion | flops 9665249280 | bytes 34603008 | tf_op jit(solution)/shard_map/tf,df->td/dot_general | solution.py:95
  240.0 0.0 reduce-scatter.2.cloned.1.call-update
  240.0 0.0 all-gather.8.cloned.1.call-start
  240.1 0.5 all-gather.8.cloned.1.call-update
  240.6 0.0 all-gather.6.cloned.1.call-start
  240.6 0.5 all-gather.6.cloned.1.call-update
  241.2 3.6 fusion.51
  244.8 4.0 copy.42
  248.8 3.2 all_to_all.46
  252.0 4.7 all-to-all-start.1
  256.7 4.0 fusion.72
  260.7 1.9 copy.96
  262.6 14.6 %all-to-all-done.1 = bf16[512,4,192]{0,2,1:T(8,128)(2,1)} async-done(((bf16[512,4,192]{0,2,1:T(8,128)(2,1)}), bf16[512,4,192]{0,2,1:T(8,128)(2,1)}, u32[]{:S(2)}, u32[]{:S(2)}) %all-to-all-start.1) | async-done | bytes 786464 | tf_op jit(solution)/shard_map/all_to_all | solution.py:113
  277.2 4.9 %all-to-all-start = ((bf16[512,4,768]{2,0,1:T(8,128)(2,1)}), bf16[512,4,768]{2,0,1:T(8,128)(2,1)}, u32[]{:S(2)}, u32[]{:S(2)}) async-start(bf16[512,4,768]{2,0,1:T(8,128)(2,1)} %bitcast.146), calls=%async_computation.1 | async-start | bytes 6291456 | tf_op jit(solution)/shard_map/all_to_all | solution.py:112
  282.1 0.1 dynamic-slice.3
  282.2 2.1 copy.59
  284.3 1.9 copy.95
  286.2 67.0 %all-to-all-done = bf16[512,4,768]{2,0,1:T(8,128)(2,1)} async-done(((bf16[512,4,768]{2,0,1:T(8,128)(2,1)}), bf16[512,4,768]{2,0,1:T(8,128)(2,1)}, u32[]{:S(2)}, u32[]{:S(2)}) %all-to-all-start) | async-done | bytes 3145760 | tf_op jit(solution)/shard_map/all_to_all | solution.py:112
  353.2 4.7 all-to-all-start.2
  357.9 0.0 all-gather.4.cloned.1.call-done
  357.9 13.2 %convolution_convert_fusion.2 = bf16[768,2304]{1,0:T(8,128)(2,1)} fusion(bf16[2048,768]{1,0:T(8,128)(2,1)} %bitcast.11, bf16[2048,2304]{0,1:T(8,128)(2,1)} %all-gather.4.cloned.1.call-done), kind=kOutput, calls=%fused_computation.22 | convolution fusion | flops 7249526784 | bytes 16121856 | tf_op jit(solution)/shard_map/td,ta->da/dot_general | solution.py:119
  371.1 4.5 copy.40
  375.6 3.7 copy.45
  379.3 2.7 fusion.79
  382.1 5.1 %all-reduce = (f32[128]{0:T(128)S(1)}, f32[128]{0:T(128)S(1)}) all-reduce(f32[128]{0:T(128)S(1)} %get-tuple-element.18, f32[128]{0:T(128)S(1)} %get-tuple-element.17), channel_id=1, replica_groups=mesh['dp'=4,'row'=2,'col'=4] {'row'}, use_global_device_ids=true, to_apply=%region_20.0 | all-reduce | flops 256 | bytes 2048 | tf_op jit(solution)/shard_map/psum | solution.py:104
  387.2 3.2 add_convert_fusion
  390.4 8.2 %fusion.14 = bf16[1,1,192,3072]{3,2,1,0:T(8,128)(2,1)} fusion(bf16[2048,192]{0,1:T(8,128)(2,1)S(1)} %bitcast.154, bf16[2048,3072]{1,0:T(8,128)(2,1)} %all-gather.8.cloned.1.call-done), kind=kOutput, calls=%fused_computation.27 | convolution fusion | flops 2416508928 | bytes 14548992 | tf_op jit(solution)/shard_map/ta,td->ad/dot_general | solution.py:121
  398.6 11.4 %all-to-all-done.2 = bf16[512,4,768]{2,0,1:T(8,128)(2,1)} async-done(((bf16[512,4,768]{2,0,1:T(8,128)(2,1)}), bf16[512,4,768]{2,0,1:T(8,128)(2,1)}, u32[]{:S(2)}, u32[]{:S(2)}) %all-to-all-start.2) | async-done | bytes 3145760 | tf_op jit(solution)/shard_map/all_to_all | solution.py:114
  410.0 15.5 %fusion.13 = bf16[1,1,768,3072]{3,2,1,0:T(8,128)(2,1)} fusion(bf16[2048,768]{1,0:T(8,128)(2,1)} %bitcast.19, bf16[2048,3072]{1,0:T(8,128)(2,1)} %all-gather.8.cloned.1.call-done), kind=kOutput, calls=%fused_computation.25 | convolution fusion | flops 9666035712 | bytes 20447232 | tf_op jit(solution)/shard_map/tf,td->fd/dot_general | solution.py:122
  425.5 41.8 %all-gather.6.cloned.1.call-done = bf16[2048,3072]{1,0:T(8,128)(2,1)} async-done(((bf16[512,3072]{1,0:T(8,128)(2,1)}), bf16[2048,3072]{1,0:T(8,128)(2,1)}) %all-gather.6.cloned.1.call-update) | async-done | bytes 12582928 | tf_op jit(solution)/shard_map/all_gather | solution.py:118
  467.3 15.3 %fusion.12 = bf16[1,1,768,3072]{3,2,1,0:T(8,128)(2,1)} fusion(bf16[2048,768]{1,0:T(8,128)(2,1)} %bitcast.11, bf16[2048,3072]{1,0:T(8,128)(2,1)} %all-gather.6.cloned.1.call-done), kind=kOutput, calls=%fused_computation.24 | convolution fusion | flops 9666035712 | bytes 20447232 | tf_op jit(solution)/shard_map/td,tf->df/dot_general | solution.py:120
  (34 shorter events, 0.1 us)
Async XLA Ops:
  8.0 206.6 %all-reduce.5.cloned.1.call-start = ((), (), s32[]{:S(2)}) async-start(), calls=%async_computation.4 | async-start | bytes 12582912 | tf_op jit(solution)/shard_map/psum | solution.py:74
  24.4 7.3 %copy-start = (bf16[512,3072]{1,0:T(8,128)(2,1)S(1)}, bf16[512,3072]{1,0:T(8,128)(2,1)}, u32[]{:S(2)}) copy-start(bf16[512,3072]{1,0:T(8,128)(2,1)} %param.8) | copy-start | bytes 9437188
  24.5 333.5 %all-gather.4.cloned.1.call-start = ((), (), s32[]{:S(2)}) async-start(), calls=%async_computation.6 | async-start | bytes 11796480 | tf_op jit(solution)/shard_map/all_gather | solution.py:117
  124.9 2.9 copy-start.6
  145.9 2.2 copy-start.8
  145.9 3.3 copy-start.10
  154.6 19.5 %copy-start.4 = (bf16[288,8,2,256]{3,1,2,0:T(8,128)(2,1)S(1)}, bf16[288,8,2,256]{3,1,2,0:T(8,128)(2,1)}, u32[]{:S(2)}) copy-start(bf16[288,8,2,256]{3,1,2,0:T(8,128)(2,1)} %copy.60) | copy-start | bytes 7077892
  154.6 224.7 %reduce-scatter.2.cloned.1.call-start = ((), (), s32[]{:S(2)}) async-start(), calls=%async_computation.5 | async-start | bytes 7864320 | tf_op jit(solution)/shard_map/reduce_scatter | solution.py:94
  222.4 17.5 %copy-start.2 = (bf16[512,3072]{1,0:T(8,128)(2,1)}, bf16[512,3072]{1,0:T(8,128)(2,1)S(1)}, u32[]{:S(2)}) copy-start(bf16[512,3072]{1,0:T(8,128)(2,1)S(1)} %get-tuple-element.31) | copy-start | bytes 9437188
  240.0 1.2 copy-start.7
  240.0 150.4 %all-gather.8.cloned.1.call-start = ((), (), s32[]{:S(2)}) async-start(), calls=%async_computation.8 | async-start | bytes 15728640 | tf_op jit(solution)/shard_map/all_gather | solution.py:116
  240.6 226.7 %all-gather.6.cloned.1.call-start = ((), (), s32[]{:S(2)}) async-start(), calls=%async_computation.7 | async-start | bytes 15728640 | tf_op jit(solution)/shard_map/all_gather | solution.py:118
  244.8 11.9 %copy-start.1 = (bf16[512,3072]{1,0:T(8,128)(2,1)S(1)}, bf16[512,3072]{1,0:T(8,128)(2,1)}, u32[]{:S(2)}) copy-start(bf16[512,3072]{1,0:T(8,128)(2,1)} %param.8) | copy-start | bytes 9437188
  252.0 25.2 %all-to-all-start.1 = ((bf16[512,4,192]{0,2,1:T(8,128)(2,1)}), bf16[512,4,192]{0,2,1:T(8,128)(2,1)}, u32[]{:S(2)}, u32[]{:S(2)}) async-start(bf16[512,4,192]{0,2,1:T(8,128)(2,1)} %all_to_all.46), calls=%async_computation.2 | async-start | bytes 1572864 | tf_op jit(solution)/shard_map/all_to_all | solution.py:113
  277.2 7.1 %copy-start.3 = (bf16[512,3072]{1,0:T(8,128)(2,1)S(1)}, bf16[512,3072]{1,0:T(8,128)(2,1)}, u32[]{:S(2)}) copy-start(bf16[512,3072]{1,0:T(8,128)(2,1)} %get-tuple-element.30) | copy-start | bytes 9437188
  277.2 76.0 %all-to-all-start = ((bf16[512,4,768]{2,0,1:T(8,128)(2,1)}), bf16[512,4,768]{2,0,1:T(8,128)(2,1)}, u32[]{:S(2)}, u32[]{:S(2)}) async-start(bf16[512,4,768]{2,0,1:T(8,128)(2,1)} %bitcast.146), calls=%async_computation.1 | async-start | bytes 6291456 | tf_op jit(solution)/shard_map/all_to_all | solution.py:112
  353.2 56.7 %all-to-all-start.2 = ((bf16[512,4,768]{2,0,1:T(8,128)(2,1)}), bf16[512,4,768]{2,0,1:T(8,128)(2,1)}, u32[]{:S(2)}, u32[]{:S(2)}) async-start(bf16[512,4,768]{2,0,1:T(8,128)(2,1)} %bitcast.145), calls=%async_computation.3 | async-start | bytes 6291456 | tf_op jit(solution)/shard_map/all_to_all | solution.py:114
  379.3 7.8 %copy-start.5 = (f32[128,3072]{1,0:T(8,128)S(1)}, f32[128,3072]{1,0:T(8,128)}, u32[]{:S(2)}) copy-start(f32[128,3072]{1,0:T(8,128)} %reduce-scatter.2.cloned.1.call-done) | copy-start | bytes 4718596
  382.1 8.3 %copy-start.9 = (bf16[4,24,8,512]{3,2,0,1:T(8,128)(2,1)S(1)}, bf16[4,24,8,512]{3,2,0,1:T(8,128)(2,1)}, u32[]{:S(2)}) copy-start(bf16[4,24,8,512]{3,2,0,1:T(8,128)(2,1)} %copy.59) | copy-start | bytes 2359300
Sparse Core Ops, SparseCore 0:
  24.6 190.0 all-reduce.4
  240.1 110.7 reduce-scatter.1
Sparse Core Ops, SparseCore 1:
  154.7 64.6 all-gather.3
  242.0 127.3 all-gather.7
  371.4 95.8 all-gather.5
where the time goes:
time: 499 us; the launch traced here: 490 us
  waiting for transfers between devices  164 us (33%)
  matrix products  131 us (26%)
  blocking collectives  84.5 us (17%)
  local copies, waits for them, and re-layouts  58.4 us (12%)
  other arithmetic  22.3 us (4%)
  between operations  16.1 us (3%)
  starting transfers between devices  14.5 us (3%)
    psum x1, blocking collectives, body(): sum_attn, sum_hidden = lax.psum((part_attn, part_hidden), 'row')  79.4 us
    all_to_all x1, waiting for transfers between devices, body(): lax.all_to_all(normed_b, 'dp', split_axis=1, concat_axis=0, tiled=True)  67 us
    all_gather x1, waiting for transfers between devices, body(): pre_piece = lax.all_gather(grad_pre, 'dp', axis=0, tiled=True)  41.8 us
    unnamed x27, local copies, waits for them, and re-layouts  31 us
    psum x1, waiting for transfers between devices, body(): sum_attn, sum_hidden = lax.psum((part_attn, part_hidden), 'row')  27.9 us
    dot_general x1, matrix products, body(): jnp.einsum('tf,df->td', grad_pre, weight_up, preferred_element_type=f32)  17.5 us
    dot_general x1, matrix products, body(): jnp.einsum('td,fd->tf', cotangent, weight_down, preferred_element_type=f32)  16.4 us
    dot_general x1, matrix products, body(): jnp.einsum('tf,td->fd', moved_hidden, cot_piece, preferred_element_type=f32)  15.5 us
  transfers between devices with their start and end apart: 8, of which 5 were waited for; matrix products, arithmetic and copies ran while one was open for 36% of the time, Pallas kernels for 0%

commit v1 on v0

--- a/solution.py
+++ b/solution.py
@@ -115,9 +115,23 @@
     )
     cot_piece = lax.all_gather(cotangent, "dp", axis=0, tiled=True)
     flat_piece = lax.all_gather(grad_flat, "dp", axis=0, tiled=True)
-    pre_piece = lax.all_gather(grad_pre, "dp", axis=0, tiled=True)
     new_qkv = jnp.einsum("td,ta->da", moved_normed, flat_piece, preferred_element_type=f32)
-    new_up = jnp.einsum("td,tf->df", moved_normed, pre_piece, preferred_element_type=f32)
+    count, here, rows = (lax.axis_size("dp"), lax.axis_index("dp"), grad_pre.shape[0])
+    right = [(i, (i + 1) % count) for i in range(count)]
+    held, total_2 = (grad_pre, None)
+    for step in range(count):
+        coming = lax.ppermute(held, "dp", right) if step < count - 1 else None
+        update = jnp.einsum(
+            "td,tf->df",
+            lax.dynamic_slice_in_dim(
+                moved_normed, (here - step) % count * rows, held.shape[0], axis=0
+            ),
+            held,
+            preferred_element_type=f32,
+        )
+        total_2 = update if total_2 is None else total_2 + update
+        held = coming
+    new_up = total_2
     new_attn = jnp.einsum("ta,td->ad", moved_attended, cot_piece, preferred_element_type=f32)
     new_down = jnp.einsum("tf,td->fd", moved_hidden, cot_piece, preferred_element_type=f32)
     grad_qkv = new_qkv.astype(bf16).reshape(1, 1, new_qkv.shape[0], 3, head_cols)

time: 499 us -> 539 us (1.080)
  matrix products: 131 us -> 156 us
  starting transfers between devices: 14.5 us -> 27.1 us
    ppermute x0 -> x3, waiting for transfers between devices: none -> 128 us  [body(): coming = lax.ppermute(held, 'dp', right) if step < count - 1 else None]
    all_to_all x1, waiting for transfers between devices: 67 us -> 8.42 us  [body(): lax.all_to_all(normed_b, 'dp', split_axis=1, concat_axis=0, tiled=True)]
    all_gather x1 -> x0, waiting for transfers between devices: 41.8 us -> none  [body(): pre_piece = lax.all_gather(grad_pre, 'dp', axis=0, tiled=True)]
    dot_general x1 -> x4, matrix products: 15.3 us -> 41 us  [body(): jnp.einsum('td,tf->df', lax.dynamic_slice_in_dim(moved_normed, (here - st...]
    all_to_all x1, waiting for transfers between devices: 14.6 us -> 0.01 us  [body(): lax.all_to_all(attended, 'dp', split_axis=1, concat_axis=0, tiled=True)]
    all_to_all x1, waiting for transfers between devices: 11.4 us -> 0.01 us  [body(): lax.all_to_all(hidden_b, 'dp', split_axis=1, concat_axis=0, tiled=True)]
    all_to_all x1, starting transfers between devices: 4.66 us -> 10.8 us  [body(): lax.all_to_all(hidden_b, 'dp', split_axis=1, concat_axis=0, tiled=True)]
    all_to_all x1, starting transfers between devices: 4.93 us -> 10.4 us  [body(): lax.all_to_all(normed_b, 'dp', split_axis=1, concat_axis=0, tiled=True)]
  transfers between devices with their start and end apart: 8 -> 10, of which waited for: 5 -> 5; matrix products, arithmetic and copies ran while one was open for 36% -> 37% of each run, Pallas kernels for 0% -> 0%
where the time goes in v1:
time: 539 us; the launch traced here: 530 us
  waiting for transfers between devices  165 us (31%)
  matrix products  156 us (29%)
  blocking collectives  84.4 us (16%)
  local copies, waits for them, and re-layouts  59.1 us (11%)
  starting transfers between devices  27.1 us (5%)
  other arithmetic  22.6 us (4%)
  between operations  16 us (3%)
    ppermute x3, waiting for transfers between devices, body(): coming = lax.ppermute(held, 'dp', right) if step < count - 1 else None  128 us
    psum x1, blocking collectives, body(): sum_attn, sum_hidden = lax.psum((part_attn, part_hidden), 'row')  79.4 us
    dot_general x4, matrix products, body(): jnp.einsum('td,tf->df', lax.dynamic_slice_in_dim(moved_normed, (here - st...  41 us
    unnamed x25, local copies, waits for them, and re-layouts  31.8 us
    psum x1, waiting for transfers between devices, body(): sum_attn, sum_hidden = lax.psum((part_attn, part_hidden), 'row')  27.9 us
    dot_general x1, matrix products, body(): jnp.einsum('tf,df->td', grad_pre, weight_up, preferred_element_type=f32)  17.3 us
    dot_general x1, matrix products, body(): jnp.einsum('td,fd->tf', cotangent, weight_down, preferred_element_type=f32)  16.4 us
    dot_general x1, matrix products, body(): jnp.einsum('tf,td->fd', moved_hidden, cot_piece, preferred_element_type=f32)  15.4 us
  transfers between devices with their start and end apart: 10, of which 5 were waited for; matrix products, arithmetic and copies ran while one was open for 37% of the time, Pallas kernels for 0%

profile of v1, /device:TPU:0, one launch (start us, length us, event | category | flops | bytes accessed | tf_op | source)
XLA Modules:
  0.0 529.7 jit_solution(7635151967474739453)
XLA Ops:
  8.0 16.4 %fusion.98 = f32[512,3072]{1,0:T(8,128)} fusion(bf16[512,3072]{1,0:T(8,128)(2,1)} %param.11, bf16[3072,3072]{1,0:T(8,128)(2,1)} %param.15), kind=kOutput, calls=%fused_computation.121 | convolution fusion | flops 9663676416 | bytes 28311552 | tf_op jit(solution)/shard_map/td,fd->tf/dot_general | solution.py:73
  24.5 0.0 all-gather.3.cloned.1.call-start
  24.5 7.2 %fusion.96 = f32[512,768]{1,0:T(8,128)} fusion(bf16[512,3072]{1,0:T(8,128)(2,1)} %param.11, bf16[768,3072]{1,0:T(8,128)(2,1)} %param.14), kind=kOutput, calls=%fused_computation.119 | convolution fusion | flops 2415919104 | bytes 9437184 | tf_op jit(solution)/shard_map/td,ad->ta/dot_general | solution.py:72
  31.7 1.0 convert_reduce_fusion
  32.7 79.4 %all-reduce.6 = (bf16[512,768]{1,0:T(8,128)(2,1)S(1)}, f32[512]{0:T(512)S(1)}, f32[512]{0:T(512)S(1)}) all-reduce(f32[512,768]{1,0:T(8,128)} %fusion.96, f32[512]{0:T(512)S(1)} %get-tuple-element.16, f32[512]{0:T(512)S(1)} %get-tuple-element.15), channel_id=1, replica_groups=mesh['dp'=4,'row'=2,'col'=4] {'row'}, use_global_device_ids=true, to_apply=%region_9.0 | all-reduce | flops 394240 | bytes 2367488 | tf_op jit(solution)/shard_map/psum | solution.py:74
  112.2 0.9 reshape.107
  113.1 0.6 copy.35
  113.7 2.8 copy.25
  116.5 2.1 reshape.99
  118.7 3.8 fusion.91
  122.4 2.5 copy.54
  124.9 0.2 convert_reduce_fusion.1
  125.1 0.2 fusion.47
  125.3 0.2 fusion.36
  125.6 2.2 fusion.55
  127.8 2.5 fusion.17
  130.4 7.8 %bitcast_reduce_fusion = (f32[2,256,6]{1,2,0:T(8,128)S(1)}, f32[2,256,6]{1,2,0:T(8,128)S(1)}, f32[2,6,128,256]{3,2,1,0:T(8,128)}) fusion(f32[2,256,6]{1,2,0:T(8,128)S(1)} %add_rsqrt_fusion, f32[2,256,6]{1,2,0:T(8,128)S(1)} %broadcast_multiply_fusion.4, bf16[2,256,1,6,128]{1,0,4,3,2:T(2,128)(2,1)S(1)} %get-tuple-element.34, f32[2,6,256,256]{2,3,1,0:T(8,128)} %fusion.55, ...), kind=kOutput, calls=%fused_computation.66 | convolution fusion | flops 212333824 | bytes 9523200 | tf_op jit(solution)/shard_map/bhqk,bqhd->bkhd/dot_general | solution.py:85
  138.2 7.7 %bitcast_reduce_fusion.1 = (f32[2,256,6]{1,2,0:T(8,128)S(1)}, f32[2,256,6]{1,2,0:T(8,128)S(1)}, f32[2,6,128,256]{3,2,1,0:T(8,128)}) fusion(f32[2,256,6]{1,2,0:T(8,128)S(1)} %add_rsqrt_fusion.1, f32[2,256,6]{1,2,0:T(8,128)S(1)} %broadcast_multiply_fusion.5, bf16[2,256,1,6,128]{1,0,4,3,2:T(2,128)(2,1)S(1)} %get-tuple-element.33, ...), kind=kOutput, calls=%fused_computation.68 | convolution fusion | flops 212333824 | bytes 9523200 | tf_op jit(solution)/shard_map/bhqk,bkhd->bqhd/dot_general | solution.py:84
  145.8 2.1 fusion.52
  148.0 0.1 copy-done.7
  148.1 0.4 fusion.53
  148.5 0.7 copy-done.9
  149.2 0.8 fusion.50
  149.9 0.3 pad_maximum_fusion
  150.2 2.4 copy.37
  152.7 1.8 copy.60
  154.5 0.0 reduce-scatter.2.cloned.1.call-start
  154.6 19.5 %copy.38 = bf16[3072,3,768]{0,2,1:T(8,128)(2,1)} copy(bf16[3072,3,768]{2,0,1:T(8,128)(2,1)} %param.12) | data formatting | bytes 28311552 | tf_op args[4]
  174.1 12.7 %fusion.97 = f32[512,3072]{1,0:T(8,128)} fusion(bf16[512,2304]{0,1:T(8,128)(2,1)S(1)} %bitcast.154, bf16[3072,2304]{0,1:T(8,128)(2,1)} %bitcast.149), kind=kOutput, calls=%fused_computation.120 | convolution fusion | flops 7247757312 | bytes 22806528 | tf_op jit(solution)/shard_map/ta,da->td/dot_general | solution.py:93
  186.8 27.9 %all-reduce.5.cloned.1.call-done = f32[512,3072]{1,0:T(8,128)} async-done(((f32[512,3072]{1,0:T(8,128)}), f32[512,3072]{1,0:T(8,128)}) %all-reduce.5.cloned.1.call-update) | async-done | bytes 6291472 | tf_op jit(solution)/shard_map/psum | solution.py:74
  214.6 8.9 %fusion.11 = (bf16[512,3072]{1,0:T(8,128)(2,1)}, bf16[512,3072]{1,0:T(8,128)(2,1)}) fusion(bf16[512,3072]{1,0:T(8,128)(2,1)} %param.10, f32[512,3072]{1,0:T(8,128)} %all-reduce.5.cloned.1.call-done), kind=kLoop, calls=%fused_computation.20 | loop fusion | flops 22020096 | bytes 15728640 | tf_op jit(solution)/shard_map/convert_element_type | solution.py:71
  223.5 17.3 %convolution_add_fusion = f32[512,3072]{1,0:T(8,128)} fusion(f32[512,3072]{1,0:T(8,128)} %fusion.97, bf16[512,3072]{1,0:T(8,128)(2,1)} %get-tuple-element.31, bf16[3072,3072]{1,0:T(8,128)(2,1)} %param.13), kind=kOutput, calls=%fused_computation.23 | convolution fusion | flops 9665249280 | bytes 34603008 | tf_op jit(solution)/shard_map/tf,df->td/dot_general | solution.py:95
  240.9 0.0 all-gather.5.cloned.1.call-start
  240.9 0.5 all-gather.5.cloned.1.call-update
  241.5 0.1 collective-permute-start
  241.5 0.5 copy-done.6
  242.0 3.6 fusion.51
  245.6 3.9 copy.42
  249.5 3.2 all_to_all.46
  252.7 4.3 all-to-all-start.1
  257.0 71.3 %collective-permute-done = bf16[512,3072]{1,0:T(8,128)(2,1)} collective-permute-done((bf16[512,3072]{1,0:T(8,128)(2,1)}, bf16[512,3072]{1,0:T(8,128)(2,1)}, u32[]{:S(2)}, u32[]{:S(2)}) %collective-permute-start) | collective-permute-done | bytes 3145760 | tf_op jit(solution)/shard_map/ppermute | solution.py:123
  328.3 1.4 collective-permute-start.1
  329.8 4.0 fusion.83
  333.8 1.9 copy.96
  335.6 10.4 %all-to-all-start = ((bf16[512,4,768]{2,0,1:T(8,128)(2,1)}), bf16[512,4,768]{2,0,1:T(8,128)(2,1)}, u32[]{:S(2)}, u32[]{:S(2)}) async-start(bf16[512,4,768]{2,0,1:T(8,128)(2,1)} %bitcast.148), calls=%async_computation.1 | async-start | bytes 6291456 | tf_op jit(solution)/shard_map/all_to_all | solution.py:112
  346.0 0.1 dynamic-slice.3
  346.1 2.1 copy.59
  348.2 1.9 copy.95
  350.1 54.8 %collective-permute-done.1 = bf16[512,3072]{1,0:T(8,128)(2,1)} collective-permute-done((bf16[512,3072]{1,0:T(8,128)(2,1)}, bf16[512,3072]{1,0:T(8,128)(2,1)}, u32[]{:S(2)}, u32[]{:S(2)}) %collective-permute-start.1) | collective-permute-done | bytes 3145760 | tf_op jit(solution)/shard_map/ppermute | solution.py:123
  404.9 8.4 %all-to-all-done = bf16[512,4,768]{2,0,1:T(8,128)(2,1)} async-done(((bf16[512,4,768]{2,0,1:T(8,128)(2,1)}), bf16[512,4,768]{2,0,1:T(8,128)(2,1)}, u32[]{:S(2)}, u32[]{:S(2)}) %all-to-all-start) | async-done | bytes 3145760 | tf_op jit(solution)/shard_map/all_to_all | solution.py:112
  413.3 10.8 %all-to-all-start.2 = ((bf16[512,4,768]{2,0,1:T(8,128)(2,1)}), bf16[512,4,768]{2,0,1:T(8,128)(2,1)}, u32[]{:S(2)}, u32[]{:S(2)}) async-start(bf16[512,4,768]{2,0,1:T(8,128)(2,1)} %bitcast.147), calls=%async_computation.3 | async-start | bytes 6291456 | tf_op jit(solution)/shard_map/all_to_all | solution.py:114
  424.1 8.4 %fusion.62 = f32[768,3072]{1,0:T(8,128)} fusion(bf16[512,3072]{1,0:T(8,128)(2,1)} %get-tuple-element.31, bf16[2048,768]{1,0:T(8,128)(2,1)} %bitcast.11, s32[]{:T(128)S(6)} %select_n.38), kind=kOutput, calls=%fused_computation.87 | convolution fusion | flops 2415919104 | bytes 13369348 | tf_op jit(solution)/shard_map/td,tf->df/dot_general | solution.py:124
  432.5 8.3 %fusion.60 = f32[768,3072]{1,0:T(8,128)} fusion(bf16[512,3072]{1,0:T(8,128)(2,1)} %collective-permute-done, bf16[2048,768]{1,0:T(8,128)(2,1)} %bitcast.11, s32[]{:T(128)S(6)} %select_n.40), kind=kOutput, calls=%fused_computation.85 | convolution fusion | flops 2415919104 | bytes 13369348 | tf_op jit(solution)/shard_map/td,tf->df/dot_general | solution.py:124
  440.8 8.4 %fusion.58 = f32[768,3072]{1,0:T(8,128)} fusion(bf16[512,3072]{1,0:T(8,128)(2,1)} %collective-permute-done.1, bf16[2048,768]{1,0:T(8,128)(2,1)} %bitcast.11, s32[]{:T(128)S(6)} %select_n.42), kind=kOutput, calls=%fused_computation.83 | convolution fusion | flops 2415919104 | bytes 13369348 | tf_op jit(solution)/shard_map/td,tf->df/dot_general | solution.py:124
  449.3 13.2 %convolution_convert_fusion.1 = bf16[768,2304]{1,0:T(8,128)(2,1)} fusion(bf16[2048,768]{1,0:T(8,128)(2,1)} %bitcast.11, bf16[2048,2304]{0,1:T(8,128)(2,1)} %all-gather.3.cloned.1.call-done), kind=kOutput, calls=%fused_computation.22 | convolution fusion | flops 7249526784 | bytes 16121856 | tf_op jit(solution)/shard_map/td,ta->da/dot_general | solution.py:118
  462.4 4.5 copy.40
  466.9 3.9 copy.45
  470.8 1.5 collective-permute-done.2
  472.3 15.9 %fusion.13 = bf16[1,1,768,3072]{3,2,1,0:T(8,128)(2,1)} fusion(bf16[512,3072]{1,0:T(8,128)(2,1)} %collective-permute-done.2, f32[768,3072]{1,0:T(8,128)} %fusion.58, f32[768,3072]{1,0:T(8,128)} %fusion.62, f32[768,3072]{1,0:T(8,128)} %fusion.60, bf16[2048,768]{1,0:T(8,128)(2,1)} %bitcast.11, s32[]{:T(128)S(6)} %select_n.44), kind=kOutput, calls=%fused_computation.25 | convolution fusion | flops 2425356288 | bytes 36962308 | tf_op jit(solution)/shard_map/td,tf->df/dot_general | solution.py:124
  488.2 2.2 fusion.90
  490.4 4.9 all-reduce
  495.4 8.2 %fusion.14 = bf16[1,1,192,3072]{3,2,1,0:T(8,128)(2,1)} fusion(bf16[2048,192]{0,1:T(8,128)(2,1)S(1)} %bitcast.156, bf16[2048,3072]{1,0:T(8,128)(2,1)} %all-gather.5.cloned.1.call-done), kind=kOutput, calls=%fused_computation.27 | convolution fusion | flops 2416508928 | bytes 14548992 | tf_op jit(solution)/shard_map/ta,td->ad/dot_general | solution.py:135
  503.6 15.4 %fusion.12 = bf16[1,1,768,3072]{3,2,1,0:T(8,128)(2,1)} fusion(bf16[2048,768]{1,0:T(8,128)(2,1)} %bitcast.19, bf16[2048,3072]{1,0:T(8,128)(2,1)} %all-gather.5.cloned.1.call-done), kind=kOutput, calls=%fused_computation.24 | convolution fusion | flops 9666035712 | bytes 20447232 | tf_op jit(solution)/shard_map/tf,td->fd/dot_general | solution.py:136
  519.0 3.0 add_convert_fusion.1
  (38 shorter events, 0.2 us)
Async XLA Ops:
  8.0 206.6 %all-reduce.5.cloned.1.call-start = ((), (), s32[]{:S(2)}) async-start(), calls=%async_computation.4 | async-start | bytes 12582912 | tf_op jit(solution)/shard_map/psum | solution.py:74
  24.4 7.3 %copy-start = (bf16[512,3072]{1,0:T(8,128)(2,1)S(1)}, bf16[512,3072]{1,0:T(8,128)(2,1)}, u32[]{:S(2)}) copy-start(bf16[512,3072]{1,0:T(8,128)(2,1)} %param.8) | copy-start | bytes 9437188
  24.5 424.8 %all-gather.3.cloned.1.call-start = ((), (), s32[]{:S(2)}) async-start(), calls=%async_computation.6 | async-start | bytes 11796480 | tf_op jit(solution)/shard_map/all_gather | solution.py:117
  124.9 2.9 copy-start.5
  145.8 2.3 copy-start.7
  145.8 3.3 copy-start.9
  154.5 19.6 %copy-start.3 = (bf16[288,8,2,256]{3,1,2,0:T(8,128)(2,1)S(1)}, bf16[288,8,2,256]{3,1,2,0:T(8,128)(2,1)}, u32[]{:S(2)}) copy-start(bf16[288,8,2,256]{3,1,2,0:T(8,128)(2,1)} %copy.60) | copy-start | bytes 7077892
  154.5 333.7 %reduce-scatter.2.cloned.1.call-start = ((), (), s32[]{:S(2)}) async-start(), calls=%async_computation.5 | async-start | bytes 7864320 | tf_op jit(solution)/shard_map/reduce_scatter | solution.py:94
  240.8 1.1 copy-start.6
  240.9 254.5 %all-gather.5.cloned.1.call-start = ((), (), s32[]{:S(2)}) async-start(), calls=%async_computation.7 | async-start | bytes 15728640 | tf_op jit(solution)/shard_map/all_gather | solution.py:116
  241.5 86.9 %collective-permute-start = (bf16[512,3072]{1,0:T(8,128)(2,1)}, bf16[512,3072]{1,0:T(8,128)(2,1)}, u32[]{:S(2)}, u32[]{:S(2)}) collective-permute-start(bf16[512,3072]{1,0:T(8,128)(2,1)} %get-tuple-element.31), channel_id=1, source_target_pairs={{0,8},{8,16},{16,24},{24,0},{1,9},{9,17},{17,25},{25,1},{2,10},{10... | collective-permute-start | bytes 9437192 | tf_op jit(solution)/shard_map/ppermute | solution.py:123
  245.6 84.2 %copy-start.1 = (bf16[512,3072]{1,0:T(8,128)(2,1)S(1)}, bf16[512,3072]{1,0:T(8,128)(2,1)}, u32[]{:S(2)}) copy-start(bf16[512,3072]{1,0:T(8,128)(2,1)} %param.8) | copy-start | bytes 9437188
  252.7 82.9 %all-to-all-start.1 = ((bf16[512,4,192]{0,2,1:T(8,128)(2,1)}), bf16[512,4,192]{0,2,1:T(8,128)(2,1)}, u32[]{:S(2)}, u32[]{:S(2)}) async-start(bf16[512,4,192]{0,2,1:T(8,128)(2,1)} %all_to_all.46), calls=%async_computation.2 | async-start | bytes 1572864 | tf_op jit(solution)/shard_map/all_to_all | solution.py:113
  328.3 76.6 %collective-permute-start.1 = (bf16[512,3072]{1,0:T(8,128)(2,1)}, bf16[512,3072]{1,0:T(8,128)(2,1)}, u32[]{:S(2)}, u32[]{:S(2)}) collective-permute-start(bf16[512,3072]{1,0:T(8,128)(2,1)} %collective-permute-done), channel_id=1, source_target_pairs={{0,8},{8,16},{16,24},{24,0},{1,9},{9,17},{17,25},{25,1},{2,10},{10... | collective-permute-start | bytes 9437192 | tf_op jit(solution)/shard_map/ppermute | solution.py:123
  335.6 12.6 %copy-start.2 = (bf16[512,3072]{1,0:T(8,128)(2,1)S(1)}, bf16[512,3072]{1,0:T(8,128)(2,1)}, u32[]{:S(2)}) copy-start(bf16[512,3072]{1,0:T(8,128)(2,1)} %get-tuple-element.30) | copy-start | bytes 9437188
  335.6 77.7 %all-to-all-start = ((bf16[512,4,768]{2,0,1:T(8,128)(2,1)}), bf16[512,4,768]{2,0,1:T(8,128)(2,1)}, u32[]{:S(2)}, u32[]{:S(2)}) async-start(bf16[512,4,768]{2,0,1:T(8,128)(2,1)} %bitcast.148), calls=%async_computation.1 | async-start | bytes 6291456 | tf_op jit(solution)/shard_map/all_to_all | solution.py:112
  404.9 67.4 %collective-permute-start.2 = (bf16[512,3072]{1,0:T(8,128)(2,1)}, bf16[512,3072]{1,0:T(8,128)(2,1)}, u32[]{:S(2)}, u32[]{:S(2)}) collective-permute-start(bf16[512,3072]{1,0:T(8,128)(2,1)} %collective-permute-done.1), channel_id=1, source_target_pairs={{0,8},{8,16},{16,24},{24,0},{1,9},{9,17},{17,25},{25,1},{2,10},{10... | collective-permute-start | bytes 9437192 | tf_op jit(solution)/shard_map/ppermute | solution.py:123
  413.3 90.2 %all-to-all-start.2 = ((bf16[512,4,768]{2,0,1:T(8,128)(2,1)}), bf16[512,4,768]{2,0,1:T(8,128)(2,1)}, u32[]{:S(2)}, u32[]{:S(2)}) async-start(bf16[512,4,768]{2,0,1:T(8,128)(2,1)} %bitcast.147), calls=%async_computation.3 | async-start | bytes 6291456 | tf_op jit(solution)/shard_map/all_to_all | solution.py:114
  488.2 7.2 %copy-start.8 = (bf16[4,24,8,512]{3,2,0,1:T(8,128)(2,1)S(1)}, bf16[4,24,8,512]{3,2,0,1:T(8,128)(2,1)}, u32[]{:S(2)}) copy-start(bf16[4,24,8,512]{3,2,0,1:T(8,128)(2,1)} %copy.59) | copy-start | bytes 2359300
  503.6 15.4 %copy-start.4 = (f32[128,3072]{1,0:T(8,128)S(1)}, f32[128,3072]{1,0:T(8,128)}, u32[]{:S(2)}) copy-start(f32[128,3072]{1,0:T(8,128)} %reduce-scatter.2.cloned.1.call-done) | copy-start | bytes 4718596
Sparse Core Ops, SparseCore 0:
  24.6 190.0 all-reduce.4
  241.0 110.7 reduce-scatter.1
Sparse Core Ops, SparseCore 1:
  154.6 64.6 all-gather.2
  242.9 123.8 all-gather.4
